TPU v7x, 128 devices: a whole 4x4x4 slice. The times are simulated.
128 devices in a mesh: row: 8 (over x, core), col: 16 (over z, y).
Axes of the slice: x: 4, y: 4, z: 4, core: 2. Of those that a mesh axis runs over, the one named last changes fastest.
Arguments:
- right_sides: bfloat16 [32768, 12288], P('row', 'col'), may hold values from -6 to 6
- factor_panels: bfloat16 [32768, 1024], P(('row', 'col')), may hold values from -0.1875 to 0.1875
- inverse_blocks: float32 [4, 256, 256], replicated, may hold values from -1 to 1, as said below
Outputs:
- solved_sides: float32 [32768, 12288], P('row', 'col')
Inputs may be any that keep to these rules, and one draw needn't show every extreme that they name: `inverse_blocks`: each block is unit lower triangular.
All inputs are finite; a program needn't handle non-finite values.
Results may differ from a plain program's by a relative error of at most 0.003.
Values may be sent and summed in bfloat16 or wider, within the bound.
No kernel may reach another device: no remote copies, remote signals or barrier semaphores. Data moves between devices by JAX's collectives and lax.ppermute only.
A program may use at most 192 MiB of HBM per device.

v0:
```python
import jax
import jax.numpy as jnp
from jax import lax
from jax.sharding import PartitionSpec as P


def from_root(value, axis, root):
    mine = lax.axis_index(axis) == root
    return lax.psum(jnp.where(mine, value, jnp.zeros_like(value)), axis)


def publish(solved, panel_num):
    return from_root(solved.astype(jnp.bfloat16), "row", panel_num)


def per_device(right_sides, factor_panels, inverse_blocks):
    panel_count = inverse_blocks.shape[0]
    panel_width = inverse_blocks.shape[1]
    row_index = lax.axis_index("row")
    current = right_sides.astype(jnp.float32)
    for panel_num in range(panel_count):
        leading = current[:panel_width]
        solved = jnp.dot(inverse_blocks[panel_num], leading, precision=lax.Precision.HIGHEST)
        shared = publish(solved, panel_num)
        columns = factor_panels[:, panel_num * panel_width : (panel_num + 1) * panel_width]
        update = jnp.dot(
            lax.all_gather(columns, "col", axis=0, tiled=True),
            shared,
            preferred_element_type=jnp.float32,
        )
        updated_first = jnp.where(row_index > panel_num, leading - update[:panel_width], leading)
        new_first = jnp.where(row_index == panel_num, solved, updated_first)
        current = jnp.concatenate([new_first, current[panel_width:] - update[panel_width:]], 0)
    return current


def solution(mesh):
    placed = (P("row", "col"), P(("row", "col"), None), P())
    return jax.shard_map(
        per_device, mesh=mesh, in_specs=placed, out_specs=P("row", "col"), check_vma=False
    )
```

profile of v0, /device:TPU:0, one launch (start us, length us, event | category | flops | bytes accessed | tf_op | source)
XLA Modules:
  0.0 335.0 jit_solution(2568119471155261356)
XLA Ops:
  7.4 0.0 all-reduce.5.cloned.1.call-start
  7.4 2.3 convert_select_fusion.3
  9.7 0.0 all-reduce.5.cloned.1.call-update
  9.7 0.0 all-gather.5.cloned.1.call-start
  9.8 1.9 fusion.14
  11.7 0.0 all-gather.5.cloned.1.call-update
  11.7 0.0 all-gather.7.cloned.1.call-start
  11.7 0.5 all-gather.7.cloned.1.call-update
  12.3 0.0 all-reduce.7.cloned.1.call-start
  12.3 8.6 %convert_element_type.15 = f32[4096,768]{1,0:T(8,128)} convert(bf16[4096,768]{1,0:T(8,128)(2,1)} %param.3) | non-fusion elementwise | flops 3145728 | bytes 18874368 | tf_op jit(solution)/shard_map/convert_element_type | solution.py:20
  20.9 0.0 copy-start.3
  20.9 53.2 %all-reduce.5.cloned.1.call-done = bf16[256,768]{1,0:T(8,128)(2,1)} async-done(((bf16[256,768]{1,0:T(8,128)(2,1)}), bf16[256,768]{1,0:T(8,128)(2,1)}) %all-reduce.5.cloned.1.call-update) | async-done | bytes 393232 | tf_op jit(solution)/shard_map/psum | solution.py:9
  74.1 0.0 all-gather.5.cloned.1.call-done
  74.1 3.4 %convolution_bitcast_fusion.3 = f32[4096,768]{1,0:T(8,128)S(1)} fusion(bf16[4096,256]{1,0:T(8,128)(2,1)} %all-gather.5.cloned.1.call-done, bf16[256,768]{1,0:T(8,128)(2,1)} %all-reduce.5.cloned.1.call-done), kind=kOutput, calls=%fused_computation.8 | convolution fusion | flops 1610612736 | bytes 15073280 | tf_op jit(solution)/shard_map/dot_general | solution.py:26
  77.5 0.0 copy-start
  77.5 4.5 %copy-done = f32[4096,768]{1,0:T(8,128)} copy-done((f32[4096,768]{1,0:T(8,128)}, f32[4096,768]{1,0:T(8,128)S(1)}, u32[]{:S(2)}) %copy-start) | copy-done | bytes 12582936
  82.0 1.3 fusion
  83.3 0.0 copy-done.3
  83.3 1.6 convert_select_fusion.2
  85.0 0.0 all-reduce.7.cloned.1.call-update
  85.0 0.0 all-gather.9.cloned.1.call-start
  85.0 0.5 all-gather.9.cloned.1.call-update
  85.6 0.0 all-reduce.9.cloned.1.call-start
  85.6 20.7 %all-gather.7.cloned.1.call-done = bf16[4096,256]{1,0:T(8,128)(2,1)} async-done(((bf16[256,256]{1,0:T(8,128)(2,1)}), bf16[4096,256]{1,0:T(8,128)(2,1)}) %all-gather.7.cloned.1.call-update) | async-done | bytes 2097168 | tf_op jit(solution)/shard_map/all_gather | solution.py:27
  106.3 38.7 %all-reduce.7.cloned.1.call-done = bf16[256,768]{1,0:T(8,128)(2,1)} async-done(((bf16[256,768]{1,0:T(8,128)(2,1)}), bf16[256,768]{1,0:T(8,128)(2,1)}) %all-reduce.7.cloned.1.call-update) | async-done | bytes 393232 | tf_op jit(solution)/shard_map/psum | solution.py:9
  145.0 3.4 %convolution_bitcast_fusion.2 = f32[4096,768]{1,0:T(8,128)S(1)} fusion(bf16[4096,256]{1,0:T(8,128)(2,1)} %all-gather.7.cloned.1.call-done, bf16[256,768]{1,0:T(8,128)(2,1)} %all-reduce.7.cloned.1.call-done), kind=kOutput, calls=%fused_computation.7 | convolution fusion | flops 1610612736 | bytes 15073280 | tf_op jit(solution)/shard_map/dot_general | solution.py:26
  148.5 0.0 copy-start.1
  148.5 4.5 %copy-done.1 = f32[4096,768]{1,0:T(8,128)} copy-done((f32[4096,768]{1,0:T(8,128)}, f32[4096,768]{1,0:T(8,128)S(1)}, u32[]{:S(2)}) %copy-start.1) | copy-done | bytes 12582936
  153.0 0.1 fusion.1
  153.1 1.6 convert_select_fusion.1
  154.7 0.0 all-reduce.9.cloned.1.call-update
  154.8 0.0 all-gather.11.cloned.1.call-start
  154.8 0.7 all-gather.11.cloned.1.call-update
  155.5 0.2 all-reduce.11.cloned.1.call-start
  155.7 0.0 all-gather.9.cloned.1.call-done
  155.8 59.4 %all-reduce.9.cloned.1.call-done = bf16[256,768]{1,0:T(8,128)(2,1)} async-done(((bf16[256,768]{1,0:T(8,128)(2,1)}), bf16[256,768]{1,0:T(8,128)(2,1)}) %all-reduce.9.cloned.1.call-update) | async-done | bytes 393232 | tf_op jit(solution)/shard_map/psum | solution.py:9
  215.2 3.4 %convolution_bitcast_fusion.1 = f32[4096,768]{1,0:T(8,128)S(1)} fusion(bf16[4096,256]{1,0:T(8,128)(2,1)} %all-gather.9.cloned.1.call-done, bf16[256,768]{1,0:T(8,128)(2,1)} %all-reduce.9.cloned.1.call-done), kind=kOutput, calls=%fused_computation.6 | convolution fusion | flops 1610612736 | bytes 15073280 | tf_op jit(solution)/shard_map/dot_general | solution.py:26
  218.6 0.0 copy-start.2
  218.6 4.6 %copy-done.2 = f32[4096,768]{1,0:T(8,128)} copy-done((f32[4096,768]{1,0:T(8,128)}, f32[4096,768]{1,0:T(8,128)S(1)}, u32[]{:S(2)}) %copy-start.2) | copy-done | bytes 12582936
  223.2 0.1 fusion.2
  223.3 1.6 convert_select_fusion
  224.9 0.0 all-reduce.11.cloned.1.call-update
  225.0 0.0 all-gather.11.cloned.1.call-done
  225.0 59.6 %all-reduce.11.cloned.1.call-done = bf16[256,768]{1,0:T(8,128)(2,1)} async-done(((bf16[256,768]{1,0:T(8,128)(2,1)}), bf16[256,768]{1,0:T(8,128)(2,1)}) %all-reduce.11.cloned.1.call-update) | async-done | bytes 393232 | tf_op jit(solution)/shard_map/psum | solution.py:9
  284.6 7.9 %convolution_bitcast_fusion = f32[4096,768]{1,0:T(8,128)} fusion(bf16[4096,256]{1,0:T(8,128)(2,1)} %all-gather.11.cloned.1.call-done, bf16[256,768]{1,0:T(8,128)(2,1)} %all-reduce.11.cloned.1.call-done), kind=kOutput, calls=%fused_computation.5 | convolution fusion | flops 1610612736 | bytes 15073280 | tf_op jit(solution)/shard_map/dot_general | solution.py:26
  292.5 24.0 %slice_subtract_fusion = f32[3840,768]{1,0:T(8,128)} fusion(f32[4096,768]{1,0:T(8,128)} %convolution_bitcast_fusion, f32[4096,768]{1,0:T(8,128)} %copy-done.2, f32[4096,768]{1,0:T(8,128)} %copy-done.1, f32[4096,768]{1,0:T(8,128)} %copy-done, f32[4096,768]{1,0:T(8,128)} %convert_element_type.15), kind=kLoop, calls=%fused_computation.1 | loop fusion | flops 11796480 | bytes 70778880 | tf_op jit(solution)/shard_map/sub | solution.py:33
  316.5 1.3 fusion.3
  317.7 9.9 %pad_maximum_fusion = f32[4096,768]{1,0:T(8,128)} fusion(f32[3840,768]{1,0:T(8,128)} %slice_subtract_fusion, f32[256,768]{1,0:T(8,128)S(1)} %fusion.3), kind=kLoop, calls=%fused_computation | loop fusion | flops 3145728 | bytes 25165824 | tf_op jit(solution)/shard_map/concatenate | solution.py:33
Async XLA Ops:
  7.4 66.7 %all-reduce.5.cloned.1.call-start = ((), (), s32[]{:S(2)}) async-start(), calls=%async_computation | async-start | bytes 786432 | tf_op jit(solution)/shard_map/psum | solution.py:9
  9.7 64.4 %all-gather.5.cloned.1.call-start = ((), (), s32[]{:S(2)}) async-start(), calls=%async_computation.1 | async-start | bytes 2228224 | tf_op jit(solution)/shard_map/all_gather | solution.py:27
  11.7 94.7 %all-gather.7.cloned.1.call-start = ((), (), s32[]{:S(2)}) async-start(), calls=%async_computation.3 | async-start | bytes 2228224 | tf_op jit(solution)/shard_map/all_gather | solution.py:27
  12.3 132.8 %all-reduce.7.cloned.1.call-start = ((), (), s32[]{:S(2)}) async-start(), calls=%async_computation.2 | async-start | bytes 786432 | tf_op jit(solution)/shard_map/psum | solution.py:9
  20.9 62.4 %copy-start.3 = (f32[4,256,256]{2,1,0:T(8,128)S(1)}, f32[4,256,256]{2,1,0:T(8,128)}, u32[]{:S(2)}) copy-start(f32[4,256,256]{2,1,0:T(8,128)} %param.5) | copy-start | bytes 3145732
  77.5 4.5 %copy-start = (f32[4096,768]{1,0:T(8,128)}, f32[4096,768]{1,0:T(8,128)S(1)}, u32[]{:S(2)}) copy-start(f32[4096,768]{1,0:T(8,128)S(1)} %convolution_bitcast_fusion.3) | copy-start | bytes 37748740
  85.0 70.8 %all-gather.9.cloned.1.call-start = ((), (), s32[]{:S(2)}) async-start(), calls=%async_computation.5 | async-start | bytes 2228224 | tf_op jit(solution)/shard_map/all_gather | solution.py:27
  85.6 129.6 %all-reduce.9.cloned.1.call-start = ((), (), s32[]{:S(2)}) async-start(), calls=%async_computation.4 | async-start | bytes 786432 | tf_op jit(solution)/shard_map/psum | solution.py:9
  148.5 4.5 %copy-start.1 = (f32[4096,768]{1,0:T(8,128)}, f32[4096,768]{1,0:T(8,128)S(1)}, u32[]{:S(2)}) copy-start(f32[4096,768]{1,0:T(8,128)S(1)} %convolution_bitcast_fusion.2) | copy-start | bytes 37748740
  154.8 70.2 %all-gather.11.cloned.1.call-start = ((), (), s32[]{:S(2)}) async-start(), calls=%async_computation.7 | async-start | bytes 2228224 | tf_op jit(solution)/shard_map/all_gather | solution.py:27
  155.5 129.1 %all-reduce.11.cloned.1.call-start = ((), (), s32[]{:S(2)}) async-start(), calls=%async_computation.6 | async-start | bytes 786432 | tf_op jit(solution)/shard_map/psum | solution.py:9
  218.6 4.6 %copy-start.2 = (f32[4096,768]{1,0:T(8,128)}, f32[4096,768]{1,0:T(8,128)S(1)}, u32[]{:S(2)}) copy-start(f32[4096,768]{1,0:T(8,128)S(1)} %convolution_bitcast_fusion.1) | copy-start | bytes 37748740
Sparse Core Ops, SparseCore 0:
  10.5 63.5 all-reduce.4
  85.1 59.8 all-reduce.6
  154.9 60.2 all-reduce.8
  225.1 59.4 all-reduce.10
Sparse Core Ops, SparseCore 1:
  12.3 47.6 all-gather.4
  62.0 44.3 all-gather.6
  108.4 44.3 all-gather.8
  157.7 44.2 all-gather.10
where the time goes:
time: 335 us
  waiting for transfers between devices  233 us (70%)
  other arithmetic  45.3 us (14%)
  matrix products  25.3 us (8%)
  local copies, waits for them, and re-layouts  15.5 us (5%)
  between operations  15 us (4%)
    psum x4, waiting for transfers between devices, from_root(): return lax.psum(jnp.where(mine, value, jnp.zeros_like(value)), axis)  211 us
    sub x1, other arithmetic, per_device(): current[panel_width:] - update[panel_width:]  24 us
    all_gather x4, waiting for transfers between devices, per_device(): lax.all_gather(columns, 'col', axis=0, tiled=True)  20.8 us
    dot_general x4, matrix products, per_device(): jnp.dot(lax.all_gather(columns, 'col', axis=0, tiled=True), shared, prefe...  18.2 us
    unnamed x8, local copies, waits for them, and re-layouts  13.6 us
    concatenate x1, other arithmetic, per_device(): jnp.concatenate([new_first, current[panel_width:] - update[panel_width:]]...  9.94 us
    convert_element_type x1, other arithmetic, per_device(): current = right_sides.astype(jnp.float32)  8.55 us
    dot_general x4, matrix products, per_device(): jnp.dot(inverse_blocks[panel_num], leading, precision=lax.Precision.HIGHEST)  7.15 us
  transfers between devices with their start and end apart: 8, of which 5 were waited for; matrix products, arithmetic and copies ran while one was open for 8% of the time, Pallas kernels for 0%

commit v1 on v0

--- a/solution.py
+++ b/solution.py
@@ -2,6 +2,22 @@
 import jax.numpy as jnp
 from jax import lax
 from jax.sharding import PartitionSpec as P
+
+
+def collect(x, axis, dim):
+    ways, here, hop = (lax.axis_size(axis), lax.axis_index(axis), x.shape[dim])
+    dims = [n * ways if d == dim else n for d, n in enumerate(x.shape)]
+    full = lax.dynamic_update_slice_in_dim(jnp.zeros(dims, x.dtype), x, here * hop, axis=dim)
+    going_up = going_down = x
+    for far in range(1, ways // 2 + 1):
+        going_up = lax.ppermute(going_up, axis, [(d, (d + 1) % ways) for d in range(ways)])
+        full = lax.dynamic_update_slice_in_dim(full, going_up, (here - far) % ways * hop, axis=dim)
+        if 2 * far < ways:
+            going_down = lax.ppermute(going_down, axis, [(d, (d - 1) % ways) for d in range(ways)])
+            full = lax.dynamic_update_slice_in_dim(
+                full, going_down, (here + far) % ways * hop, axis=dim
+            )
+    return full
 
 
 def from_root(value, axis, root):
@@ -23,11 +39,7 @@
         solved = jnp.dot(inverse_blocks[panel_num], leading, precision=lax.Precision.HIGHEST)
         shared = publish(solved, panel_num)
         columns = factor_panels[:, panel_num * panel_width : (panel_num + 1) * panel_width]
-        update = jnp.dot(
-            lax.all_gather(columns, "col", axis=0, tiled=True),
-            shared,
-            preferred_element_type=jnp.float32,
-        )
+        update = jnp.dot(collect(columns, "col", 0), shared, preferred_element_type=jnp.float32)
         updated_first = jnp.where(row_index > panel_num, leading - update[:panel_width], leading)
         new_first = jnp.where(row_index == panel_num, solved, updated_first)
         current = jnp.concatenate([new_first, current[panel_width:] - update[panel_width:]], 0)

time: 335 us -> 489 us (1.46); the launches traced: 335 us -> 480 us
  starting transfers between devices: 0.48 us -> 151 us
  waiting for transfers between devices: 233 us -> 187 us
  local copies, waits for them, and re-layouts: 15.5 us -> 55 us
    ppermute x0 -> x60, starting transfers between devices: none -> 151 us  [the longest x28 149 us: collect(): lax.ppermute(going_down, axis, [(d, (d - 1) % ways) for d in range(ways)])]
    dynamic_update_slice x0 -> x63, local copies, waits for them, and re-layouts: none -> 37 us  [the longest x32 20.7 us: collect(): lax.dynamic_update_slice_in_dim(full, going_up, (here - far) % ways * hop...]
    psum x4, waiting for transfers between devices: 211 us -> 175 us  [from_root(): return lax.psum(jnp.where(mine, value, jnp.zeros_like(value)), axis)]
    all_gather x4 -> x0, waiting for transfers between devices: 20.8 us -> none  [per_device(): lax.all_gather(columns, 'col', axis=0, tiled=True)]
    ppermute x0 -> x60, waiting for transfers between devices: none -> 11.8 us  [the longest x32 11.7 us: collect(): lax.ppermute(going_up, axis, [(d, (d + 1) % ways) for d in range(ways)])]
    unnamed x8 -> x16, local copies, waits for them, and re-layouts: 13.6 us -> 14.6 us
  transfers between devices with their start and end apart: 8 -> 64, of which waited for: 5 -> 6; matrix products, arithmetic and copies ran while one was open for 8% -> 15% of each run, Pallas kernels for 0% -> 0%
where the time goes in v1:
time: 489 us; the launch traced here: 480 us
  waiting for transfers between devices  187 us (38%)
  starting transfers between devices  151 us (31%)
  local copies, waits for them, and re-layouts  55 us (11%)
  other arithmetic  45.4 us (9%)
  matrix products  27.8 us (6%)
  between operations  13.8 us (3%)
    psum x4, waiting for transfers between devices, from_root(): return lax.psum(jnp.where(mine, value, jnp.zeros_like(value)), axis)  175 us
    ppermute x28, starting transfers between devices, collect(): lax.ppermute(going_down, axis, [(d, (d - 1) % ways) for d in range(ways)])  149 us
    sub x1, other arithmetic, per_device(): current[panel_width:] - update[panel_width:]  24 us
    dynamic_update_slice x32, local copies, waits for them, and re-layouts, collect(): lax.dynamic_update_slice_in_dim(full, going_up, (here - far) % ways * hop...  20.7 us
    dot_general x4, matrix products, per_device(): jnp.dot(collect(columns, 'col', 0), shared, preferred_element_type=jnp.fl...  17.1 us
    dynamic_update_slice x28, local copies, waits for them, and re-layouts, collect(): lax.dynamic_update_slice_in_dim(full, going_down, (here + far) % ways * h...  15 us
    unnamed x16, local copies, waits for them, and re-layouts  14.6 us
    ppermute x32, waiting for transfers between devices, collect(): lax.ppermute(going_up, axis, [(d, (d + 1) % ways) for d in range(ways)])  11.7 us
  transfers between devices with their start and end apart: 64, of which 6 were waited for; matrix products, arithmetic and copies ran while one was open for 15% of the time, Pallas kernels for 0%

profile of v1, /device:TPU:0, one launch (start us, length us, event | category | flops | bytes accessed | tf_op | source)
XLA Modules:
  0.0 479.6 jit_solution(5531491535178529010)
XLA Ops:
  6.7 0.9 copy-done.7
  7.6 1.8 collective-permute-start.15
  9.4 5.0 %collective-permute-start.16 = (bf16[256,256]{1,0:T(8,128)(2,1)S(1)}, bf16[256,256]{1,0:T(8,128)(2,1)S(1)}, u32[]{:S(2)}, u32[]{:S(2)}) collective-permute-start(bf16[256,256]{1,0:T(8,128)(2,1)S(1)} %get-tuple-element.7), channel_id=1, source_target_pairs={{0,15},{1,0},{2,1},{3,2},{4,3},{5,4},{6,5},{7,6},{8,7},{9,8},{10,9... | collective-permute-start | bytes 393224 | tf_op jit(solution)/shard_map/ppermute | solution.py:16
  14.4 5.3 %collective-permute-start.1 = (bf16[256,256]{1,0:T(8,128)(2,1)S(1)}, bf16[256,256]{1,0:T(8,128)(2,1)S(1)}, u32[]{:S(2)}, u32[]{:S(2)}) collective-permute-start(bf16[256,256]{1,0:T(8,128)(2,1)S(1)} %get-tuple-element.8), channel_id=1, source_target_pairs={{0,15},{1,0},{2,1},{3,2},{4,3},{5,4},{6,5},{7,6},{8,7},{9,8},{10,9... | collective-permute-start | bytes 393224 | tf_op jit(solution)/shard_map/ppermute | solution.py:16
  19.7 2.6 convert_select_fusion.3
  22.6 1.5 broadcast.21.clone.3
  24.2 0.7 constant_dynamic-update-slice_fusion.31
  24.9 1.4 broadcast.21.clone
  27.0 8.6 %convert_element_type.15 = f32[4096,768]{1,0:T(8,128)} convert(bf16[4096,768]{1,0:T(8,128)(2,1)} %param.3) | non-fusion elementwise | flops 3145728 | bytes 18874368 | tf_op jit(solution)/shard_map/convert_element_type | solution.py:36
  35.5 5.3 %collective-permute-start.31 = (bf16[256,256]{1,0:T(8,128)(2,1)S(1)}, bf16[256,256]{1,0:T(8,128)(2,1)S(1)}, u32[]{:S(2)}, u32[]{:S(2)}) collective-permute-start(bf16[256,256]{1,0:T(8,128)(2,1)S(1)} %get-tuple-element.5), channel_id=1, source_target_pairs={{0,15},{1,0},{2,1},{3,2},{4,3},{5,4},{6,5},{7,6},{8,7},{9,8},{10,9... | collective-permute-start | bytes 393224 | tf_op jit(solution)/shard_map/ppermute | solution.py:16
  40.8 1.6 constant_dynamic-update-slice_fusion.46
  42.4 5.4 %collective-permute-start.46 = (bf16[256,256]{1,0:T(8,128)(2,1)S(1)}, bf16[256,256]{1,0:T(8,128)(2,1)S(1)}, u32[]{:S(2)}, u32[]{:S(2)}) collective-permute-start(bf16[256,256]{1,0:T(8,128)(2,1)S(1)} %get-tuple-element.9), channel_id=1, source_target_pairs={{0,15},{1,0},{2,1},{3,2},{4,3},{5,4},{6,5},{7,6},{8,7},{9,8},{10,9... | collective-permute-start | bytes 393224 | tf_op jit(solution)/shard_map/ppermute | solution.py:16
  48.5 5.4 %collective-permute-start.18 = (bf16[256,256]{1,0:T(8,128)(2,1)S(1)}, bf16[256,256]{1,0:T(8,128)(2,1)S(1)}, u32[]{:S(2)}, u32[]{:S(2)}) collective-permute-start(bf16[256,256]{1,0:T(8,128)(2,1)S(1)} %collective-permute-done.16), channel_id=1, source_target_pairs={{0,15},{1,0},{2,1},{3,2},{4,3},{5,4},{6,5},{7,6},{8,7},{9,8},{10,9... | collective-permute-start | bytes 393224 | tf_op jit(solution)/shard_map/ppermute | solution.py:16
  53.9 1.6 constant_dynamic-update-slice_fusion.30
  56.2 5.3 %collective-permute-start.3 = (bf16[256,256]{1,0:T(8,128)(2,1)S(1)}, bf16[256,256]{1,0:T(8,128)(2,1)S(1)}, u32[]{:S(2)}, u32[]{:S(2)}) collective-permute-start(bf16[256,256]{1,0:T(8,128)(2,1)S(1)} %collective-permute-done.1), channel_id=1, source_target_pairs={{0,15},{1,0},{2,1},{3,2},{4,3},{5,4},{6,5},{7,6},{8,7},{9,8},{10,9... | collective-permute-start | bytes 393224 | tf_op jit(solution)/shard_map/ppermute | solution.py:16
  62.8 5.3 %collective-permute-start.33 = (bf16[256,256]{1,0:T(8,128)(2,1)S(1)}, bf16[256,256]{1,0:T(8,128)(2,1)S(1)}, u32[]{:S(2)}, u32[]{:S(2)}) collective-permute-start(bf16[256,256]{1,0:T(8,128)(2,1)S(1)} %collective-permute-done.31), channel_id=1, source_target_pairs={{0,15},{1,0},{2,1},{3,2},{4,3},{5,4},{6,5},{7,6},{8,7},{9,8},{10,9... | collective-permute-start | bytes 393224 | tf_op jit(solution)/shard_map/ppermute | solution.py:16
  68.9 5.4 %collective-permute-start.48 = (bf16[256,256]{1,0:T(8,128)(2,1)S(1)}, bf16[256,256]{1,0:T(8,128)(2,1)S(1)}, u32[]{:S(2)}, u32[]{:S(2)}) collective-permute-start(bf16[256,256]{1,0:T(8,128)(2,1)S(1)} %collective-permute-done.46), channel_id=1, source_target_pairs={{0,15},{1,0},{2,1},{3,2},{4,3},{5,4},{6,5},{7,6},{8,7},{9,8},{10,9... | collective-permute-start | bytes 393224 | tf_op jit(solution)/shard_map/ppermute | solution.py:16
  74.9 5.4 %collective-permute-start.20 = (bf16[256,256]{1,0:T(8,128)(2,1)S(1)}, bf16[256,256]{1,0:T(8,128)(2,1)S(1)}, u32[]{:S(2)}, u32[]{:S(2)}) collective-permute-start(bf16[256,256]{1,0:T(8,128)(2,1)S(1)} %collective-permute-done.18), channel_id=1, source_target_pairs={{0,15},{1,0},{2,1},{3,2},{4,3},{5,4},{6,5},{7,6},{8,7},{9,8},{10,9... | collective-permute-start | bytes 393224 | tf_op jit(solution)/shard_map/ppermute | solution.py:16
  81.7 5.3 %collective-permute-start.5 = (bf16[256,256]{1,0:T(8,128)(2,1)S(1)}, bf16[256,256]{1,0:T(8,128)(2,1)S(1)}, u32[]{:S(2)}, u32[]{:S(2)}) collective-permute-start(bf16[256,256]{1,0:T(8,128)(2,1)S(1)} %collective-permute-done.3), channel_id=1, source_target_pairs={{0,15},{1,0},{2,1},{3,2},{4,3},{5,4},{6,5},{7,6},{8,7},{9,8},{10,9... | collective-permute-start | bytes 393224 | tf_op jit(solution)/shard_map/ppermute | solution.py:16
  88.3 5.4 %collective-permute-start.35 = (bf16[256,256]{1,0:T(8,128)(2,1)S(1)}, bf16[256,256]{1,0:T(8,128)(2,1)S(1)}, u32[]{:S(2)}, u32[]{:S(2)}) collective-permute-start(bf16[256,256]{1,0:T(8,128)(2,1)S(1)} %collective-permute-done.33), channel_id=1, source_target_pairs={{0,15},{1,0},{2,1},{3,2},{4,3},{5,4},{6,5},{7,6},{8,7},{9,8},{10,9... | collective-permute-start | bytes 393224 | tf_op jit(solution)/shard_map/ppermute | solution.py:16
  94.4 5.9 %collective-permute-start.50 = (bf16[256,256]{1,0:T(8,128)(2,1)S(1)}, bf16[256,256]{1,0:T(8,128)(2,1)S(1)}, u32[]{:S(2)}, u32[]{:S(2)}) collective-permute-start(bf16[256,256]{1,0:T(8,128)(2,1)S(1)} %collective-permute-done.48), channel_id=1, source_target_pairs={{0,15},{1,0},{2,1},{3,2},{4,3},{5,4},{6,5},{7,6},{8,7},{9,8},{10,9... | collective-permute-start | bytes 393224 | tf_op jit(solution)/shard_map/ppermute | solution.py:16
  101.0 5.4 %collective-permute-start.22 = (bf16[256,256]{1,0:T(8,128)(2,1)S(1)}, bf16[256,256]{1,0:T(8,128)(2,1)S(1)}, u32[]{:S(2)}, u32[]{:S(2)}) collective-permute-start(bf16[256,256]{1,0:T(8,128)(2,1)S(1)} %collective-permute-done.20), channel_id=1, source_target_pairs={{0,15},{1,0},{2,1},{3,2},{4,3},{5,4},{6,5},{7,6},{8,7},{9,8},{10,9... | collective-permute-start | bytes 393224 | tf_op jit(solution)/shard_map/ppermute | solution.py:16
  107.7 5.3 %collective-permute-start.7 = (bf16[256,256]{1,0:T(8,128)(2,1)S(1)}, bf16[256,256]{1,0:T(8,128)(2,1)S(1)}, u32[]{:S(2)}, u32[]{:S(2)}) collective-permute-start(bf16[256,256]{1,0:T(8,128)(2,1)S(1)} %collective-permute-done.5), channel_id=1, source_target_pairs={{0,15},{1,0},{2,1},{3,2},{4,3},{5,4},{6,5},{7,6},{8,7},{9,8},{10,9... | collective-permute-start | bytes 393224 | tf_op jit(solution)/shard_map/ppermute | solution.py:16
  114.4 5.3 %collective-permute-start.37 = (bf16[256,256]{1,0:T(8,128)(2,1)S(1)}, bf16[256,256]{1,0:T(8,128)(2,1)S(1)}, u32[]{:S(2)}, u32[]{:S(2)}) collective-permute-start(bf16[256,256]{1,0:T(8,128)(2,1)S(1)} %collective-permute-done.35), channel_id=1, source_target_pairs={{0,15},{1,0},{2,1},{3,2},{4,3},{5,4},{6,5},{7,6},{8,7},{9,8},{10,9... | collective-permute-start | bytes 393224 | tf_op jit(solution)/shard_map/ppermute | solution.py:16
  120.4 5.4 %collective-permute-start.52 = (bf16[256,256]{1,0:T(8,128)(2,1)S(1)}, bf16[256,256]{1,0:T(8,128)(2,1)S(1)}, u32[]{:S(2)}, u32[]{:S(2)}) collective-permute-start(bf16[256,256]{1,0:T(8,128)(2,1)S(1)} %collective-permute-done.50), channel_id=1, source_target_pairs={{0,15},{1,0},{2,1},{3,2},{4,3},{5,4},{6,5},{7,6},{8,7},{9,8},{10,9... | collective-permute-start | bytes 393224 | tf_op jit(solution)/shard_map/ppermute | solution.py:16
  126.5 5.4 %collective-permute-start.24 = (bf16[256,256]{1,0:T(8,128)(2,1)S(1)}, bf16[256,256]{1,0:T(8,128)(2,1)S(1)}, u32[]{:S(2)}, u32[]{:S(2)}) collective-permute-start(bf16[256,256]{1,0:T(8,128)(2,1)S(1)} %collective-permute-done.22), channel_id=1, source_target_pairs={{0,15},{1,0},{2,1},{3,2},{4,3},{5,4},{6,5},{7,6},{8,7},{9,8},{10,9... | collective-permute-start | bytes 393224 | tf_op jit(solution)/shard_map/ppermute | solution.py:16
  133.2 5.3 %collective-permute-start.9 = (bf16[256,256]{1,0:T(8,128)(2,1)S(1)}, bf16[256,256]{1,0:T(8,128)(2,1)S(1)}, u32[]{:S(2)}, u32[]{:S(2)}) collective-permute-start(bf16[256,256]{1,0:T(8,128)(2,1)S(1)} %collective-permute-done.7), channel_id=1, source_target_pairs={{0,15},{1,0},{2,1},{3,2},{4,3},{5,4},{6,5},{7,6},{8,7},{9,8},{10,9... | collective-permute-start | bytes 393224 | tf_op jit(solution)/shard_map/ppermute | solution.py:16
  139.9 5.4 %collective-permute-start.39 = (bf16[256,256]{1,0:T(8,128)(2,1)S(1)}, bf16[256,256]{1,0:T(8,128)(2,1)S(1)}, u32[]{:S(2)}, u32[]{:S(2)}) collective-permute-start(bf16[256,256]{1,0:T(8,128)(2,1)S(1)} %collective-permute-done.37), channel_id=1, source_target_pairs={{0,15},{1,0},{2,1},{3,2},{4,3},{5,4},{6,5},{7,6},{8,7},{9,8},{10,9... | collective-permute-start | bytes 393224 | tf_op jit(solution)/shard_map/ppermute | solution.py:16
  145.9 5.4 %collective-permute-start.54 = (bf16[256,256]{1,0:T(8,128)(2,1)S(1)}, bf16[256,256]{1,0:T(8,128)(2,1)S(1)}, u32[]{:S(2)}, u32[]{:S(2)}) collective-permute-start(bf16[256,256]{1,0:T(8,128)(2,1)S(1)} %collective-permute-done.52), channel_id=1, source_target_pairs={{0,15},{1,0},{2,1},{3,2},{4,3},{5,4},{6,5},{7,6},{8,7},{9,8},{10,9... | collective-permute-start | bytes 393224 | tf_op jit(solution)/shard_map/ppermute | solution.py:16
  152.0 5.4 %collective-permute-start.26 = (bf16[256,256]{1,0:T(8,128)(2,1)S(1)}, bf16[256,256]{1,0:T(8,128)(2,1)S(1)}, u32[]{:S(2)}, u32[]{:S(2)}) collective-permute-start(bf16[256,256]{1,0:T(8,128)(2,1)S(1)} %collective-permute-done.24), channel_id=1, source_target_pairs={{0,15},{1,0},{2,1},{3,2},{4,3},{5,4},{6,5},{7,6},{8,7},{9,8},{10,9... | collective-permute-start | bytes 393224 | tf_op jit(solution)/shard_map/ppermute | solution.py:16
  157.4 0.7 constant_dynamic-update-slice_fusion.22
  158.8 5.3 %collective-permute-start.11 = (bf16[256,256]{1,0:T(8,128)(2,1)S(1)}, bf16[256,256]{1,0:T(8,128)(2,1)S(1)}, u32[]{:S(2)}, u32[]{:S(2)}) collective-permute-start(bf16[256,256]{1,0:T(8,128)(2,1)S(1)} %collective-permute-done.9), channel_id=1, source_target_pairs={{0,15},{1,0},{2,1},{3,2},{4,3},{5,4},{6,5},{7,6},{8,7},{9,8},{10,9... | collective-permute-start | bytes 393224 | tf_op jit(solution)/shard_map/ppermute | solution.py:16
  165.4 5.3 %collective-permute-start.41 = (bf16[256,256]{1,0:T(8,128)(2,1)S(1)}, bf16[256,256]{1,0:T(8,128)(2,1)S(1)}, u32[]{:S(2)}, u32[]{:S(2)}) collective-permute-start(bf16[256,256]{1,0:T(8,128)(2,1)S(1)} %collective-permute-done.39), channel_id=1, source_target_pairs={{0,15},{1,0},{2,1},{3,2},{4,3},{5,4},{6,5},{7,6},{8,7},{9,8},{10,9... | collective-permute-start | bytes 393224 | tf_op jit(solution)/shard_map/ppermute | solution.py:16
  171.5 5.4 %collective-permute-start.56 = (bf16[256,256]{1,0:T(8,128)(2,1)S(1)}, bf16[256,256]{1,0:T(8,128)(2,1)S(1)}, u32[]{:S(2)}, u32[]{:S(2)}) collective-permute-start(bf16[256,256]{1,0:T(8,128)(2,1)S(1)} %collective-permute-done.54), channel_id=1, source_target_pairs={{0,15},{1,0},{2,1},{3,2},{4,3},{5,4},{6,5},{7,6},{8,7},{9,8},{10,9... | collective-permute-start | bytes 393224 | tf_op jit(solution)/shard_map/ppermute | solution.py:16
  177.6 5.4 %collective-permute-start.28 = (bf16[256,256]{1,0:T(8,128)(2,1)S(1)}, bf16[256,256]{1,0:T(8,128)(2,1)}, u32[]{:S(2)}, u32[]{:S(2)}) collective-permute-start(bf16[256,256]{1,0:T(8,128)(2,1)S(1)} %collective-permute-done.26), channel_id=1, source_target_pairs={{0,15},{1,0},{2,1},{3,2},{4,3},{5,4},{6,5},{7,6},{8,7},{9,8},{10,9... | collective-permute-start | bytes 393224 | tf_op jit(solution)/shard_map/ppermute | solution.py:16
  184.3 5.4 %collective-permute-start.13 = (bf16[256,256]{1,0:T(8,128)(2,1)S(1)}, bf16[256,256]{1,0:T(8,128)(2,1)S(1)}, u32[]{:S(2)}, u32[]{:S(2)}) collective-permute-start(bf16[256,256]{1,0:T(8,128)(2,1)S(1)} %collective-permute-done.11), channel_id=1, source_target_pairs={{0,15},{1,0},{2,1},{3,2},{4,3},{5,4},{6,5},{7,6},{8,7},{9,8},{10,9... | collective-permute-start | bytes 393224 | tf_op jit(solution)/shard_map/ppermute | solution.py:16
  191.0 5.3 %collective-permute-start.43 = (bf16[256,256]{1,0:T(8,128)(2,1)S(1)}, bf16[256,256]{1,0:T(8,128)(2,1)}, u32[]{:S(2)}, u32[]{:S(2)}) collective-permute-start(bf16[256,256]{1,0:T(8,128)(2,1)S(1)} %collective-permute-done.41), channel_id=1, source_target_pairs={{0,15},{1,0},{2,1},{3,2},{4,3},{5,4},{6,5},{7,6},{8,7},{9,8},{10,9... | collective-permute-start | bytes 393224 | tf_op jit(solution)/shard_map/ppermute | solution.py:16
  196.3 1.6 constant_dynamic-update-slice_fusion.34
  198.1 2.0 collective-permute-done.42
  200.1 3.4 collective-permute-start.58
  203.5 1.6 constant_dynamic-update-slice_fusion.18
  205.0 2.0 collective-permute-done.57
  207.7 7.6 %collective-permute-done.14 = bf16[256,256]{1,0:T(8,128)(2,1)S(1)} collective-permute-done((bf16[256,256]{1,0:T(8,128)(2,1)S(1)}, bf16[256,256]{1,0:T(8,128)(2,1)S(1)}, u32[]{:S(2)}, u32[]{:S(2)}) %collective-permute-start.14) | collective-permute-done | bytes 131104 | tf_op jit(solution)/shard_map/ppermute | solution.py:13
  215.4 2.9 fusion.15
  218.3 4.6 copy-done
  222.8 1.3 fusion
  224.1 3.0 convert_select_fusion.2
  227.3 0.9 constant_dynamic-update-slice_fusion.33
  228.2 0.9 constant_dynamic-update-slice_fusion.32
  229.1 59.8 %all-reduce.7.cloned.1.call-done = bf16[256,768]{1,0:T(8,128)(2,1)} async-done(((bf16[256,768]{1,0:T(8,128)(2,1)}), bf16[256,768]{1,0:T(8,128)(2,1)}) %all-reduce.7.cloned.1.call-update) | async-done | bytes 393232 | tf_op jit(solution)/shard_map/psum | solution.py:25
  288.9 2.9 fusion.16
  291.8 4.6 copy-done.1
  296.5 2.5 convert_select_fusion.1
  299.4 1.6 constant_dynamic-update-slice_fusion.17
  301.0 1.6 constant_dynamic-update-slice_fusion.16
  302.5 56.5 %all-reduce.9.cloned.1.call-done = bf16[256,768]{1,0:T(8,128)(2,1)} async-done(((bf16[256,768]{1,0:T(8,128)(2,1)}), bf16[256,768]{1,0:T(8,128)(2,1)}) %all-reduce.9.cloned.1.call-update) | async-done | bytes 393232 | tf_op jit(solution)/shard_map/psum | solution.py:25
  359.0 3.4 fusion.17
  362.5 4.6 copy-done.2
  367.2 2.5 convert_select_fusion
  371.1 58.6 %all-reduce.11.cloned.1.call-done = bf16[256,768]{1,0:T(8,128)(2,1)} async-done(((bf16[256,768]{1,0:T(8,128)(2,1)}), bf16[256,768]{1,0:T(8,128)(2,1)}) %all-reduce.11.cloned.1.call-update) | async-done | bytes 393232 | tf_op jit(solution)/shard_map/psum | solution.py:25
  429.7 8.0 %fusion.18 = f32[4096,768]{1,0:T(8,128)} fusion(bf16[4096,256]{1,0:T(8,128)(2,1)} %constant_dynamic-update-slice_fusion, bf16[256,768]{1,0:T(8,128)(2,1)} %all-reduce.11.cloned.1.call-done), kind=kOutput, calls=%fused_computation.98 | convolution fusion | flops 1610612736 | bytes 15073280 | tf_op jit(solution)/shard_map/dot_general | solution.py:42
  437.7 24.0 %slice_subtract_fusion = f32[3840,768]{1,0:T(8,128)} fusion(f32[4096,768]{1,0:T(8,128)} %fusion.18, f32[4096,768]{1,0:T(8,128)} %copy-done.2, f32[4096,768]{1,0:T(8,128)} %copy-done.1, f32[4096,768]{1,0:T(8,128)} %copy-done, f32[4096,768]{1,0:T(8,128)} %convert_element_type.15), kind=kLoop, calls=%fused_computation.1 | loop fusion | flops 11796480 | bytes 70778880 | tf_op jit(solution)/shard_map/sub | solution.py:45
  461.7 1.3 fusion.3
  462.9 9.9 %pad_maximum_fusion = f32[4096,768]{1,0:T(8,128)} fusion(f32[3840,768]{1,0:T(8,128)} %slice_subtract_fusion, f32[256,768]{1,0:T(8,128)S(1)} %fusion.3), kind=kLoop, calls=%fused_computation | loop fusion | flops 3145728 | bytes 25165824 | tf_op jit(solution)/shard_map/concatenate | solution.py:45
  (167 shorter events, 26.1 us)
Async XLA Ops:
  6.5 208.8 %all-reduce.5.cloned.1.call-start = ((), (), s32[]{:S(2)}) async-start(), calls=%async_computation | async-start | bytes 786432 | tf_op jit(solution)/shard_map/psum | solution.py:25
  7.6 27.9 %collective-permute-start.15 = (bf16[256,256]{1,0:T(8,128)(2,1)S(1)}, bf16[256,256]{1,0:T(8,128)(2,1)}, u32[]{:S(2)}, u32[]{:S(2)}) collective-permute-start(bf16[256,256]{1,0:T(8,128)(2,1)S(1)} %get-tuple-element.7), channel_id=1, source_target_pairs={{0,1},{1,2},{2,3},{3,4},{4,5},{5,6},{6,7},{7,8},{8,9},{9,10},{10,1... | collective-permute-start | bytes 393224 | tf_op jit(solution)/shard_map/ppermute | solution.py:13
  9.4 33.0 %collective-permute-start.16 = (bf16[256,256]{1,0:T(8,128)(2,1)S(1)}, bf16[256,256]{1,0:T(8,128)(2,1)S(1)}, u32[]{:S(2)}, u32[]{:S(2)}) collective-permute-start(bf16[256,256]{1,0:T(8,128)(2,1)S(1)} %get-tuple-element.7), channel_id=1, source_target_pairs={{0,15},{1,0},{2,1},{3,2},{4,3},{5,4},{6,5},{7,6},{8,7},{9,8},{10,9... | collective-permute-start | bytes 393224 | tf_op jit(solution)/shard_map/ppermute | solution.py:16
  14.4 28.0 %collective-permute-start = (bf16[256,256]{1,0:T(8,128)(2,1)S(1)}, bf16[256,256]{1,0:T(8,128)(2,1)S(1)}, u32[]{:S(2)}, u32[]{:S(2)}) collective-permute-start(bf16[256,256]{1,0:T(8,128)(2,1)S(1)} %get-tuple-element.8), channel_id=1, source_target_pairs={{0,1},{1,2},{2,3},{3,4},{4,5},{5,6},{6,7},{7,8},{8,9},{9,10},{10,1... | collective-permute-start | bytes 393224 | tf_op jit(solution)/shard_map/ppermute | solution.py:13
  14.4 34.1 %collective-permute-start.1 = (bf16[256,256]{1,0:T(8,128)(2,1)S(1)}, bf16[256,256]{1,0:T(8,128)(2,1)S(1)}, u32[]{:S(2)}, u32[]{:S(2)}) collective-permute-start(bf16[256,256]{1,0:T(8,128)(2,1)S(1)} %get-tuple-element.8), channel_id=1, source_target_pairs={{0,15},{1,0},{2,1},{3,2},{4,3},{5,4},{6,5},{7,6},{8,7},{9,8},{10,9... | collective-permute-start | bytes 393224 | tf_op jit(solution)/shard_map/ppermute | solution.py:16
  22.3 266.6 %all-reduce.7.cloned.1.call-start = ((), (), s32[]{:S(2)}) async-start(), calls=%async_computation.1 | async-start | bytes 786432 | tf_op jit(solution)/shard_map/psum | solution.py:25
  22.4 26.1 %collective-permute-start.30 = (bf16[256,256]{1,0:T(8,128)(2,1)S(1)}, bf16[256,256]{1,0:T(8,128)(2,1)}, u32[]{:S(2)}, u32[]{:S(2)}) collective-permute-start(bf16[256,256]{1,0:T(8,128)(2,1)S(1)} %get-tuple-element.5), channel_id=1, source_target_pairs={{0,1},{1,2},{2,3},{3,4},{4,5},{5,6},{6,7},{7,8},{8,9},{9,10},{10,1... | collective-permute-start | bytes 393224 | tf_op jit(solution)/shard_map/ppermute | solution.py:13
  35.5 20.0 %collective-permute-start.31 = (bf16[256,256]{1,0:T(8,128)(2,1)S(1)}, bf16[256,256]{1,0:T(8,128)(2,1)S(1)}, u32[]{:S(2)}, u32[]{:S(2)}) collective-permute-start(bf16[256,256]{1,0:T(8,128)(2,1)S(1)} %get-tuple-element.5), channel_id=1, source_target_pairs={{0,15},{1,0},{2,1},{3,2},{4,3},{5,4},{6,5},{7,6},{8,7},{9,8},{10,9... | collective-permute-start | bytes 393224 | tf_op jit(solution)/shard_map/ppermute | solution.py:16
  42.4 13.8 %collective-permute-start.45 = (bf16[256,256]{1,0:T(8,128)(2,1)S(1)}, bf16[256,256]{1,0:T(8,128)(2,1)S(1)}, u32[]{:S(2)}, u32[]{:S(2)}) collective-permute-start(bf16[256,256]{1,0:T(8,128)(2,1)S(1)} %get-tuple-element.9), channel_id=1, source_target_pairs={{0,1},{1,2},{2,3},{3,4},{4,5},{5,6},{6,7},{7,8},{8,9},{9,10},{10,1... | collective-permute-start | bytes 393224 | tf_op jit(solution)/shard_map/ppermute | solution.py:13
  42.4 19.7 %collective-permute-start.46 = (bf16[256,256]{1,0:T(8,128)(2,1)S(1)}, bf16[256,256]{1,0:T(8,128)(2,1)S(1)}, u32[]{:S(2)}, u32[]{:S(2)}) collective-permute-start(bf16[256,256]{1,0:T(8,128)(2,1)S(1)} %get-tuple-element.9), channel_id=1, source_target_pairs={{0,15},{1,0},{2,1},{3,2},{4,3},{5,4},{6,5},{7,6},{8,7},{9,8},{10,9... | collective-permute-start | bytes 393224 | tf_op jit(solution)/shard_map/ppermute | solution.py:16
  48.5 14.3 %collective-permute-start.17 = (bf16[256,256]{1,0:T(8,128)(2,1)}, bf16[256,256]{1,0:T(8,128)(2,1)S(1)}, u32[]{:S(2)}, u32[]{:S(2)}) collective-permute-start(bf16[256,256]{1,0:T(8,128)(2,1)} %collective-permute-done.15), channel_id=1, source_target_pairs={{0,1},{1,2},{2,3},{3,4},{4,5},{5,6},{6,7},{7,8},{8,9},{9,10},{10,1... | collective-permute-start | bytes 393224 | tf_op jit(solution)/shard_map/ppermute | solution.py:13
  48.5 20.3 %collective-permute-start.18 = (bf16[256,256]{1,0:T(8,128)(2,1)S(1)}, bf16[256,256]{1,0:T(8,128)(2,1)S(1)}, u32[]{:S(2)}, u32[]{:S(2)}) collective-permute-start(bf16[256,256]{1,0:T(8,128)(2,1)S(1)} %collective-permute-done.16), channel_id=1, source_target_pairs={{0,15},{1,0},{2,1},{3,2},{4,3},{5,4},{6,5},{7,6},{8,7},{9,8},{10,9... | collective-permute-start | bytes 393224 | tf_op jit(solution)/shard_map/ppermute | solution.py:16
  55.5 13.3 %collective-permute-start.2 = (bf16[256,256]{1,0:T(8,128)(2,1)S(1)}, bf16[256,256]{1,0:T(8,128)(2,1)S(1)}, u32[]{:S(2)}, u32[]{:S(2)}) collective-permute-start(bf16[256,256]{1,0:T(8,128)(2,1)S(1)} %collective-permute-done), channel_id=1, source_target_pairs={{0,1},{1,2},{2,3},{3,4},{4,5},{5,6},{6,7},{7,8},{8,9},{9,10},{10,1... | collective-permute-start | bytes 393224 | tf_op jit(solution)/shard_map/ppermute | solution.py:13
  56.2 18.8 %collective-permute-start.3 = (bf16[256,256]{1,0:T(8,128)(2,1)S(1)}, bf16[256,256]{1,0:T(8,128)(2,1)S(1)}, u32[]{:S(2)}, u32[]{:S(2)}) collective-permute-start(bf16[256,256]{1,0:T(8,128)(2,1)S(1)} %collective-permute-done.1), channel_id=1, source_target_pairs={{0,15},{1,0},{2,1},{3,2},{4,3},{5,4},{6,5},{7,6},{8,7},{9,8},{10,9... | collective-permute-start | bytes 393224 | tf_op jit(solution)/shard_map/ppermute | solution.py:16
  62.2 12.8 %collective-permute-start.32 = (bf16[256,256]{1,0:T(8,128)(2,1)}, bf16[256,256]{1,0:T(8,128)(2,1)S(1)}, u32[]{:S(2)}, u32[]{:S(2)}) collective-permute-start(bf16[256,256]{1,0:T(8,128)(2,1)} %collective-permute-done.30), channel_id=1, source_target_pairs={{0,1},{1,2},{2,3},{3,4},{4,5},{5,6},{6,7},{7,8},{8,9},{9,10},{10,1... | collective-permute-start | bytes 393224 | tf_op jit(solution)/shard_map/ppermute | solution.py:13
  62.8 18.2 %collective-permute-start.33 = (bf16[256,256]{1,0:T(8,128)(2,1)S(1)}, bf16[256,256]{1,0:T(8,128)(2,1)S(1)}, u32[]{:S(2)}, u32[]{:S(2)}) collective-permute-start(bf16[256,256]{1,0:T(8,128)(2,1)S(1)} %collective-permute-done.31), channel_id=1, source_target_pairs={{0,15},{1,0},{2,1},{3,2},{4,3},{5,4},{6,5},{7,6},{8,7},{9,8},{10,9... | collective-permute-start | bytes 393224 | tf_op jit(solution)/shard_map/ppermute | solution.py:16
  68.8 12.8 %collective-permute-start.47 = (bf16[256,256]{1,0:T(8,128)(2,1)S(1)}, bf16[256,256]{1,0:T(8,128)(2,1)S(1)}, u32[]{:S(2)}, u32[]{:S(2)}) collective-permute-start(bf16[256,256]{1,0:T(8,128)(2,1)S(1)} %collective-permute-done.45), channel_id=1, source_target_pairs={{0,1},{1,2},{2,3},{3,4},{4,5},{5,6},{6,7},{7,8},{8,9},{9,10},{10,1... | collective-permute-start | bytes 393224 | tf_op jit(solution)/shard_map/ppermute | solution.py:13
  68.9 18.8 %collective-permute-start.48 = (bf16[256,256]{1,0:T(8,128)(2,1)S(1)}, bf16[256,256]{1,0:T(8,128)(2,1)S(1)}, u32[]{:S(2)}, u32[]{:S(2)}) collective-permute-start(bf16[256,256]{1,0:T(8,128)(2,1)S(1)} %collective-permute-done.46), channel_id=1, source_target_pairs={{0,15},{1,0},{2,1},{3,2},{4,3},{5,4},{6,5},{7,6},{8,7},{9,8},{10,9... | collective-permute-start | bytes 393224 | tf_op jit(solution)/shard_map/ppermute | solution.py:16
  74.9 13.4 %collective-permute-start.19 = (bf16[256,256]{1,0:T(8,128)(2,1)S(1)}, bf16[256,256]{1,0:T(8,128)(2,1)S(1)}, u32[]{:S(2)}, u32[]{:S(2)}) collective-permute-start(bf16[256,256]{1,0:T(8,128)(2,1)S(1)} %collective-permute-done.17), channel_id=1, source_target_pairs={{0,1},{1,2},{2,3},{3,4},{4,5},{5,6},{6,7},{7,8},{8,9},{9,10},{10,1... | collective-permute-start | bytes 393224 | tf_op jit(solution)/shard_map/ppermute | solution.py:13
  74.9 19.4 %collective-permute-start.20 = (bf16[256,256]{1,0:T(8,128)(2,1)S(1)}, bf16[256,256]{1,0:T(8,128)(2,1)S(1)}, u32[]{:S(2)}, u32[]{:S(2)}) collective-permute-start(bf16[256,256]{1,0:T(8,128)(2,1)S(1)} %collective-permute-done.18), channel_id=1, source_target_pairs={{0,15},{1,0},{2,1},{3,2},{4,3},{5,4},{6,5},{7,6},{8,7},{9,8},{10,9... | collective-permute-start | bytes 393224 | tf_op jit(solution)/shard_map/ppermute | solution.py:16
  81.0 13.3 %collective-permute-start.4 = (bf16[256,256]{1,0:T(8,128)(2,1)S(1)}, bf16[256,256]{1,0:T(8,128)(2,1)S(1)}, u32[]{:S(2)}, u32[]{:S(2)}) collective-permute-start(bf16[256,256]{1,0:T(8,128)(2,1)S(1)} %collective-permute-done.2), channel_id=1, source_target_pairs={{0,1},{1,2},{2,3},{3,4},{4,5},{5,6},{6,7},{7,8},{8,9},{9,10},{10,1... | collective-permute-start | bytes 393224 | tf_op jit(solution)/shard_map/ppermute | solution.py:13
  81.7 19.2 %collective-permute-start.5 = (bf16[256,256]{1,0:T(8,128)(2,1)S(1)}, bf16[256,256]{1,0:T(8,128)(2,1)S(1)}, u32[]{:S(2)}, u32[]{:S(2)}) collective-permute-start(bf16[256,256]{1,0:T(8,128)(2,1)S(1)} %collective-permute-done.3), channel_id=1, source_target_pairs={{0,15},{1,0},{2,1},{3,2},{4,3},{5,4},{6,5},{7,6},{8,7},{9,8},{10,9... | collective-permute-start | bytes 393224 | tf_op jit(solution)/shard_map/ppermute | solution.py:16
  87.7 13.3 %collective-permute-start.34 = (bf16[256,256]{1,0:T(8,128)(2,1)S(1)}, bf16[256,256]{1,0:T(8,128)(2,1)S(1)}, u32[]{:S(2)}, u32[]{:S(2)}) collective-permute-start(bf16[256,256]{1,0:T(8,128)(2,1)S(1)} %collective-permute-done.32), channel_id=1, source_target_pairs={{0,1},{1,2},{2,3},{3,4},{4,5},{5,6},{6,7},{7,8},{8,9},{9,10},{10,1... | collective-permute-start | bytes 393224 | tf_op jit(solution)/shard_map/ppermute | solution.py:13
  88.3 18.7 %collective-permute-start.35 = (bf16[256,256]{1,0:T(8,128)(2,1)S(1)}, bf16[256,256]{1,0:T(8,128)(2,1)S(1)}, u32[]{:S(2)}, u32[]{:S(2)}) collective-permute-start(bf16[256,256]{1,0:T(8,128)(2,1)S(1)} %collective-permute-done.33), channel_id=1, source_target_pairs={{0,15},{1,0},{2,1},{3,2},{4,3},{5,4},{6,5},{7,6},{8,7},{9,8},{10,9... | collective-permute-start | bytes 393224 | tf_op jit(solution)/shard_map/ppermute | solution.py:16
  94.3 13.3 %collective-permute-start.49 = (bf16[256,256]{1,0:T(8,128)(2,1)S(1)}, bf16[256,256]{1,0:T(8,128)(2,1)S(1)}, u32[]{:S(2)}, u32[]{:S(2)}) collective-permute-start(bf16[256,256]{1,0:T(8,128)(2,1)S(1)} %collective-permute-done.47), channel_id=1, source_target_pairs={{0,1},{1,2},{2,3},{3,4},{4,5},{5,6},{6,7},{7,8},{8,9},{9,10},{10,1... | collective-permute-start | bytes 393224 | tf_op jit(solution)/shard_map/ppermute | solution.py:13
  94.4 19.3 %collective-permute-start.50 = (bf16[256,256]{1,0:T(8,128)(2,1)S(1)}, bf16[256,256]{1,0:T(8,128)(2,1)S(1)}, u32[]{:S(2)}, u32[]{:S(2)}) collective-permute-start(bf16[256,256]{1,0:T(8,128)(2,1)S(1)} %collective-permute-done.48), channel_id=1, source_target_pairs={{0,15},{1,0},{2,1},{3,2},{4,3},{5,4},{6,5},{7,6},{8,7},{9,8},{10,9... | collective-permute-start | bytes 393224 | tf_op jit(solution)/shard_map/ppermute | solution.py:16
  100.9 13.4 %collective-permute-start.21 = (bf16[256,256]{1,0:T(8,128)(2,1)S(1)}, bf16[256,256]{1,0:T(8,128)(2,1)S(1)}, u32[]{:S(2)}, u32[]{:S(2)}) collective-permute-start(bf16[256,256]{1,0:T(8,128)(2,1)S(1)} %collective-permute-done.19), channel_id=1, source_target_pairs={{0,1},{1,2},{2,3},{3,4},{4,5},{5,6},{6,7},{7,8},{8,9},{9,10},{10,1... | collective-permute-start | bytes 393224 | tf_op jit(solution)/shard_map/ppermute | solution.py:13
  101.0 19.4 %collective-permute-start.22 = (bf16[256,256]{1,0:T(8,128)(2,1)S(1)}, bf16[256,256]{1,0:T(8,128)(2,1)S(1)}, u32[]{:S(2)}, u32[]{:S(2)}) collective-permute-start(bf16[256,256]{1,0:T(8,128)(2,1)S(1)} %collective-permute-done.20), channel_id=1, source_target_pairs={{0,15},{1,0},{2,1},{3,2},{4,3},{5,4},{6,5},{7,6},{8,7},{9,8},{10,9... | collective-permute-start | bytes 393224 | tf_op jit(solution)/shard_map/ppermute | solution.py:16
  107.0 13.3 %collective-permute-start.6 = (bf16[256,256]{1,0:T(8,128)(2,1)S(1)}, bf16[256,256]{1,0:T(8,128)(2,1)S(1)}, u32[]{:S(2)}, u32[]{:S(2)}) collective-permute-start(bf16[256,256]{1,0:T(8,128)(2,1)S(1)} %collective-permute-done.4), channel_id=1, source_target_pairs={{0,1},{1,2},{2,3},{3,4},{4,5},{5,6},{6,7},{7,8},{8,9},{9,10},{10,1... | collective-permute-start | bytes 393224 | tf_op jit(solution)/shard_map/ppermute | solution.py:13
  107.7 18.8 %collective-permute-start.7 = (bf16[256,256]{1,0:T(8,128)(2,1)S(1)}, bf16[256,256]{1,0:T(8,128)(2,1)S(1)}, u32[]{:S(2)}, u32[]{:S(2)}) collective-permute-start(bf16[256,256]{1,0:T(8,128)(2,1)S(1)} %collective-permute-done.5), channel_id=1, source_target_pairs={{0,15},{1,0},{2,1},{3,2},{4,3},{5,4},{6,5},{7,6},{8,7},{9,8},{10,9... | collective-permute-start | bytes 393224 | tf_op jit(solution)/shard_map/ppermute | solution.py:16
  113.7 12.8 %collective-permute-start.36 = (bf16[256,256]{1,0:T(8,128)(2,1)S(1)}, bf16[256,256]{1,0:T(8,128)(2,1)S(1)}, u32[]{:S(2)}, u32[]{:S(2)}) collective-permute-start(bf16[256,256]{1,0:T(8,128)(2,1)S(1)} %collective-permute-done.34), channel_id=1, source_target_pairs={{0,1},{1,2},{2,3},{3,4},{4,5},{5,6},{6,7},{7,8},{8,9},{9,10},{10,1... | collective-permute-start | bytes 393224 | tf_op jit(solution)/shard_map/ppermute | solution.py:13
  114.4 18.2 %collective-permute-start.37 = (bf16[256,256]{1,0:T(8,128)(2,1)S(1)}, bf16[256,256]{1,0:T(8,128)(2,1)S(1)}, u32[]{:S(2)}, u32[]{:S(2)}) collective-permute-start(bf16[256,256]{1,0:T(8,128)(2,1)S(1)} %collective-permute-done.35), channel_id=1, source_target_pairs={{0,15},{1,0},{2,1},{3,2},{4,3},{5,4},{6,5},{7,6},{8,7},{9,8},{10,9... | collective-permute-start | bytes 393224 | tf_op jit(solution)/shard_map/ppermute | solution.py:16
  120.3 12.9 %collective-permute-start.51 = (bf16[256,256]{1,0:T(8,128)(2,1)S(1)}, bf16[256,256]{1,0:T(8,128)(2,1)S(1)}, u32[]{:S(2)}, u32[]{:S(2)}) collective-permute-start(bf16[256,256]{1,0:T(8,128)(2,1)S(1)} %collective-permute-done.49), channel_id=1, source_target_pairs={{0,1},{1,2},{2,3},{3,4},{4,5},{5,6},{6,7},{7,8},{8,9},{9,10},{10,1... | collective-permute-start | bytes 393224 | tf_op jit(solution)/shard_map/ppermute | solution.py:13
  120.4 18.8 %collective-permute-start.52 = (bf16[256,256]{1,0:T(8,128)(2,1)S(1)}, bf16[256,256]{1,0:T(8,128)(2,1)S(1)}, u32[]{:S(2)}, u32[]{:S(2)}) collective-permute-start(bf16[256,256]{1,0:T(8,128)(2,1)S(1)} %collective-permute-done.50), channel_id=1, source_target_pairs={{0,15},{1,0},{2,1},{3,2},{4,3},{5,4},{6,5},{7,6},{8,7},{9,8},{10,9... | collective-permute-start | bytes 393224 | tf_op jit(solution)/shard_map/ppermute | solution.py:16
  126.4 13.4 %collective-permute-start.23 = (bf16[256,256]{1,0:T(8,128)(2,1)S(1)}, bf16[256,256]{1,0:T(8,128)(2,1)S(1)}, u32[]{:S(2)}, u32[]{:S(2)}) collective-permute-start(bf16[256,256]{1,0:T(8,128)(2,1)S(1)} %collective-permute-done.21), channel_id=1, source_target_pairs={{0,1},{1,2},{2,3},{3,4},{4,5},{5,6},{6,7},{7,8},{8,9},{9,10},{10,1... | collective-permute-start | bytes 393224 | tf_op jit(solution)/shard_map/ppermute | solution.py:13
  126.5 19.4 %collective-permute-start.24 = (bf16[256,256]{1,0:T(8,128)(2,1)S(1)}, bf16[256,256]{1,0:T(8,128)(2,1)S(1)}, u32[]{:S(2)}, u32[]{:S(2)}) collective-permute-start(bf16[256,256]{1,0:T(8,128)(2,1)S(1)} %collective-permute-done.22), channel_id=1, source_target_pairs={{0,15},{1,0},{2,1},{3,2},{4,3},{5,4},{6,5},{7,6},{8,7},{9,8},{10,9... | collective-permute-start | bytes 393224 | tf_op jit(solution)/shard_map/ppermute | solution.py:16
  132.6 13.3 %collective-permute-start.8 = (bf16[256,256]{1,0:T(8,128)(2,1)S(1)}, bf16[256,256]{1,0:T(8,128)(2,1)S(1)}, u32[]{:S(2)}, u32[]{:S(2)}) collective-permute-start(bf16[256,256]{1,0:T(8,128)(2,1)S(1)} %collective-permute-done.6), channel_id=1, source_target_pairs={{0,1},{1,2},{2,3},{3,4},{4,5},{5,6},{6,7},{7,8},{8,9},{9,10},{10,1... | collective-permute-start | bytes 393224 | tf_op jit(solution)/shard_map/ppermute | solution.py:13
  133.2 18.8 %collective-permute-start.9 = (bf16[256,256]{1,0:T(8,128)(2,1)S(1)}, bf16[256,256]{1,0:T(8,128)(2,1)S(1)}, u32[]{:S(2)}, u32[]{:S(2)}) collective-permute-start(bf16[256,256]{1,0:T(8,128)(2,1)S(1)} %collective-permute-done.7), channel_id=1, source_target_pairs={{0,15},{1,0},{2,1},{3,2},{4,3},{5,4},{6,5},{7,6},{8,7},{9,8},{10,9... | collective-permute-start | bytes 393224 | tf_op jit(solution)/shard_map/ppermute | solution.py:16
  139.2 12.8 %collective-permute-start.38 = (bf16[256,256]{1,0:T(8,128)(2,1)S(1)}, bf16[256,256]{1,0:T(8,128)(2,1)S(1)}, u32[]{:S(2)}, u32[]{:S(2)}) collective-permute-start(bf16[256,256]{1,0:T(8,128)(2,1)S(1)} %collective-permute-done.36), channel_id=1, source_target_pairs={{0,1},{1,2},{2,3},{3,4},{4,5},{5,6},{6,7},{7,8},{8,9},{9,10},{10,1... | collective-permute-start | bytes 393224 | tf_op jit(solution)/shard_map/ppermute | solution.py:13
  139.9 18.2 %collective-permute-start.39 = (bf16[256,256]{1,0:T(8,128)(2,1)S(1)}, bf16[256,256]{1,0:T(8,128)(2,1)S(1)}, u32[]{:S(2)}, u32[]{:S(2)}) collective-permute-start(bf16[256,256]{1,0:T(8,128)(2,1)S(1)} %collective-permute-done.37), channel_id=1, source_target_pairs={{0,15},{1,0},{2,1},{3,2},{4,3},{5,4},{6,5},{7,6},{8,7},{9,8},{10,9... | collective-permute-start | bytes 393224 | tf_op jit(solution)/shard_map/ppermute | solution.py:16
  145.9 12.9 %collective-permute-start.53 = (bf16[256,256]{1,0:T(8,128)(2,1)S(1)}, bf16[256,256]{1,0:T(8,128)(2,1)S(1)}, u32[]{:S(2)}, u32[]{:S(2)}) collective-permute-start(bf16[256,256]{1,0:T(8,128)(2,1)S(1)} %collective-permute-done.51), channel_id=1, source_target_pairs={{0,1},{1,2},{2,3},{3,4},{4,5},{5,6},{6,7},{7,8},{8,9},{9,10},{10,1... | collective-permute-start | bytes 393224 | tf_op jit(solution)/shard_map/ppermute | solution.py:13
  145.9 18.9 %collective-permute-start.54 = (bf16[256,256]{1,0:T(8,128)(2,1)S(1)}, bf16[256,256]{1,0:T(8,128)(2,1)S(1)}, u32[]{:S(2)}, u32[]{:S(2)}) collective-permute-start(bf16[256,256]{1,0:T(8,128)(2,1)S(1)} %collective-permute-done.52), channel_id=1, source_target_pairs={{0,15},{1,0},{2,1},{3,2},{4,3},{5,4},{6,5},{7,6},{8,7},{9,8},{10,9... | collective-permute-start | bytes 393224 | tf_op jit(solution)/shard_map/ppermute | solution.py:16
  152.0 13.5 %collective-permute-start.25 = (bf16[256,256]{1,0:T(8,128)(2,1)S(1)}, bf16[256,256]{1,0:T(8,128)(2,1)S(1)}, u32[]{:S(2)}, u32[]{:S(2)}) collective-permute-start(bf16[256,256]{1,0:T(8,128)(2,1)S(1)} %collective-permute-done.23), channel_id=1, source_target_pairs={{0,1},{1,2},{2,3},{3,4},{4,5},{5,6},{6,7},{7,8},{8,9},{9,10},{10,1... | collective-permute-start | bytes 393224 | tf_op jit(solution)/shard_map/ppermute | solution.py:13
  152.0 19.5 %collective-permute-start.26 = (bf16[256,256]{1,0:T(8,128)(2,1)S(1)}, bf16[256,256]{1,0:T(8,128)(2,1)S(1)}, u32[]{:S(2)}, u32[]{:S(2)}) collective-permute-start(bf16[256,256]{1,0:T(8,128)(2,1)S(1)} %collective-permute-done.24), channel_id=1, source_target_pairs={{0,15},{1,0},{2,1},{3,2},{4,3},{5,4},{6,5},{7,6},{8,7},{9,8},{10,9... | collective-permute-start | bytes 393224 | tf_op jit(solution)/shard_map/ppermute | solution.py:16
  158.1 13.3 %collective-permute-start.10 = (bf16[256,256]{1,0:T(8,128)(2,1)S(1)}, bf16[256,256]{1,0:T(8,128)(2,1)S(1)}, u32[]{:S(2)}, u32[]{:S(2)}) collective-permute-start(bf16[256,256]{1,0:T(8,128)(2,1)S(1)} %collective-permute-done.8), channel_id=1, source_target_pairs={{0,1},{1,2},{2,3},{3,4},{4,5},{5,6},{6,7},{7,8},{8,9},{9,10},{10,1... | collective-permute-start | bytes 393224 | tf_op jit(solution)/shard_map/ppermute | solution.py:13
  158.8 18.8 %collective-permute-start.11 = (bf16[256,256]{1,0:T(8,128)(2,1)S(1)}, bf16[256,256]{1,0:T(8,128)(2,1)S(1)}, u32[]{:S(2)}, u32[]{:S(2)}) collective-permute-start(bf16[256,256]{1,0:T(8,128)(2,1)S(1)} %collective-permute-done.9), channel_id=1, source_target_pairs={{0,15},{1,0},{2,1},{3,2},{4,3},{5,4},{6,5},{7,6},{8,7},{9,8},{10,9... | collective-permute-start | bytes 393224 | tf_op jit(solution)/shard_map/ppermute | solution.py:16
  164.8 12.8 %collective-permute-start.40 = (bf16[256,256]{1,0:T(8,128)(2,1)S(1)}, bf16[256,256]{1,0:T(8,128)(2,1)S(1)}, u32[]{:S(2)}, u32[]{:S(2)}) collective-permute-start(bf16[256,256]{1,0:T(8,128)(2,1)S(1)} %collective-permute-done.38), channel_id=1, source_target_pairs={{0,1},{1,2},{2,3},{3,4},{4,5},{5,6},{6,7},{7,8},{8,9},{9,10},{10,1... | collective-permute-start | bytes 393224 | tf_op jit(solution)/shard_map/ppermute | solution.py:13
  165.4 18.2 %collective-permute-start.41 = (bf16[256,256]{1,0:T(8,128)(2,1)S(1)}, bf16[256,256]{1,0:T(8,128)(2,1)S(1)}, u32[]{:S(2)}, u32[]{:S(2)}) collective-permute-start(bf16[256,256]{1,0:T(8,128)(2,1)S(1)} %collective-permute-done.39), channel_id=1, source_target_pairs={{0,15},{1,0},{2,1},{3,2},{4,3},{5,4},{6,5},{7,6},{8,7},{9,8},{10,9... | collective-permute-start | bytes 393224 | tf_op jit(solution)/shard_map/ppermute | solution.py:16
  171.5 12.8 %collective-permute-start.55 = (bf16[256,256]{1,0:T(8,128)(2,1)S(1)}, bf16[256,256]{1,0:T(8,128)(2,1)S(1)}, u32[]{:S(2)}, u32[]{:S(2)}) collective-permute-start(bf16[256,256]{1,0:T(8,128)(2,1)S(1)} %collective-permute-done.53), channel_id=1, source_target_pairs={{0,1},{1,2},{2,3},{3,4},{4,5},{5,6},{6,7},{7,8},{8,9},{9,10},{10,1... | collective-permute-start | bytes 393224 | tf_op jit(solution)/shard_map/ppermute | solution.py:13
  171.5 18.8 %collective-permute-start.56 = (bf16[256,256]{1,0:T(8,128)(2,1)S(1)}, bf16[256,256]{1,0:T(8,128)(2,1)S(1)}, u32[]{:S(2)}, u32[]{:S(2)}) collective-permute-start(bf16[256,256]{1,0:T(8,128)(2,1)S(1)} %collective-permute-done.54), channel_id=1, source_target_pairs={{0,15},{1,0},{2,1},{3,2},{4,3},{5,4},{6,5},{7,6},{8,7},{9,8},{10,9... | collective-permute-start | bytes 393224 | tf_op jit(solution)/shard_map/ppermute | solution.py:16
  177.5 13.4 %collective-permute-start.27 = (bf16[256,256]{1,0:T(8,128)(2,1)S(1)}, bf16[256,256]{1,0:T(8,128)(2,1)}, u32[]{:S(2)}, u32[]{:S(2)}) collective-permute-start(bf16[256,256]{1,0:T(8,128)(2,1)S(1)} %collective-permute-done.25), channel_id=1, source_target_pairs={{0,1},{1,2},{2,3},{3,4},{4,5},{5,6},{6,7},{7,8},{8,9},{9,10},{10,1... | collective-permute-start | bytes 393224 | tf_op jit(solution)/shard_map/ppermute | solution.py:13
  177.6 49.6 %collective-permute-start.28 = (bf16[256,256]{1,0:T(8,128)(2,1)S(1)}, bf16[256,256]{1,0:T(8,128)(2,1)}, u32[]{:S(2)}, u32[]{:S(2)}) collective-permute-start(bf16[256,256]{1,0:T(8,128)(2,1)S(1)} %collective-permute-done.26), channel_id=1, source_target_pairs={{0,15},{1,0},{2,1},{3,2},{4,3},{5,4},{6,5},{7,6},{8,7},{9,8},{10,9... | collective-permute-start | bytes 393224 | tf_op jit(solution)/shard_map/ppermute | solution.py:16
  183.6 14.2 %collective-permute-start.12 = (bf16[256,256]{1,0:T(8,128)(2,1)S(1)}, bf16[256,256]{1,0:T(8,128)(2,1)S(1)}, u32[]{:S(2)}, u32[]{:S(2)}) collective-permute-start(bf16[256,256]{1,0:T(8,128)(2,1)S(1)} %collective-permute-done.10), channel_id=1, source_target_pairs={{0,1},{1,2},{2,3},{3,4},{4,5},{5,6},{6,7},{7,8},{8,9},{9,10},{10,1... | collective-permute-start | bytes 393224 | tf_op jit(solution)/shard_map/ppermute | solution.py:13
  184.3 23.4 %collective-permute-start.13 = (bf16[256,256]{1,0:T(8,128)(2,1)S(1)}, bf16[256,256]{1,0:T(8,128)(2,1)S(1)}, u32[]{:S(2)}, u32[]{:S(2)}) collective-permute-start(bf16[256,256]{1,0:T(8,128)(2,1)S(1)} %collective-permute-done.11), channel_id=1, source_target_pairs={{0,15},{1,0},{2,1},{3,2},{4,3},{5,4},{6,5},{7,6},{8,7},{9,8},{10,9... | collective-permute-start | bytes 393224 | tf_op jit(solution)/shard_map/ppermute | solution.py:16
  190.3 9.8 %collective-permute-start.42 = (bf16[256,256]{1,0:T(8,128)(2,1)S(1)}, bf16[256,256]{1,0:T(8,128)(2,1)}, u32[]{:S(2)}, u32[]{:S(2)}) collective-permute-start(bf16[256,256]{1,0:T(8,128)(2,1)S(1)} %collective-permute-done.40), channel_id=1, source_target_pairs={{0,1},{1,2},{2,3},{3,4},{4,5},{5,6},{6,7},{7,8},{8,9},{9,10},{10,1... | collective-permute-start | bytes 393224 | tf_op jit(solution)/shard_map/ppermute | solution.py:13
  191.0 108.4 %collective-permute-start.43 = (bf16[256,256]{1,0:T(8,128)(2,1)S(1)}, bf16[256,256]{1,0:T(8,128)(2,1)}, u32[]{:S(2)}, u32[]{:S(2)}) collective-permute-start(bf16[256,256]{1,0:T(8,128)(2,1)S(1)} %collective-permute-done.41), channel_id=1, source_target_pairs={{0,15},{1,0},{2,1},{3,2},{4,3},{5,4},{6,5},{7,6},{8,7},{9,8},{10,9... | collective-permute-start | bytes 393224 | tf_op jit(solution)/shard_map/ppermute | solution.py:16
  197.9 9.1 %collective-permute-start.57 = (bf16[256,256]{1,0:T(8,128)(2,1)S(1)}, bf16[256,256]{1,0:T(8,128)(2,1)S(1)}, u32[]{:S(2)}, u32[]{:S(2)}) collective-permute-start(bf16[256,256]{1,0:T(8,128)(2,1)S(1)} %collective-permute-done.55), channel_id=1, source_target_pairs={{0,1},{1,2},{2,3},{3,4},{4,5},{5,6},{6,7},{7,8},{8,9},{9,10},{10,1... | collective-permute-start | bytes 393224 | tf_op jit(solution)/shard_map/ppermute | solution.py:13
  200.1 169.7 %collective-permute-start.58 = (bf16[256,256]{1,0:T(8,128)(2,1)S(1)}, bf16[256,256]{1,0:T(8,128)(2,1)S(1)}, u32[]{:S(2)}, u32[]{:S(2)}) collective-permute-start(bf16[256,256]{1,0:T(8,128)(2,1)S(1)} %collective-permute-done.56), channel_id=1, source_target_pairs={{0,15},{1,0},{2,1},{3,2},{4,3},{5,4},{6,5},{7,6},{8,7},{9,8},{10,9... | collective-permute-start | bytes 393224 | tf_op jit(solution)/shard_map/ppermute | solution.py:16
  207.0 8.3 %collective-permute-start.14 = (bf16[256,256]{1,0:T(8,128)(2,1)S(1)}, bf16[256,256]{1,0:T(8,128)(2,1)S(1)}, u32[]{:S(2)}, u32[]{:S(2)}) collective-permute-start(bf16[256,256]{1,0:T(8,128)(2,1)S(1)} %collective-permute-done.12), channel_id=1, source_target_pairs={{0,1},{1,2},{2,3},{3,4},{4,5},{5,6},{6,7},{7,8},{8,9},{9,10},{10,1... | collective-permute-start | bytes 393224 | tf_op jit(solution)/shard_map/ppermute | solution.py:13
  207.7 20.5 %collective-permute-start.29 = (bf16[256,256]{1,0:T(8,128)(2,1)}, bf16[256,256]{1,0:T(8,128)(2,1)}, u32[]{:S(2)}, u32[]{:S(2)}) collective-permute-start(bf16[256,256]{1,0:T(8,128)(2,1)} %collective-permute-done.27), channel_id=1, source_target_pairs={{0,1},{1,2},{2,3},{3,4},{4,5},{5,6},{6,7},{7,8},{8,9},{9,10},{10,1... | collective-permute-start | bytes 393224 | tf_op jit(solution)/shard_map/ppermute | solution.py:13
  215.3 85.6 %collective-permute-start.44 = (bf16[256,256]{1,0:T(8,128)(2,1)}, bf16[256,256]{1,0:T(8,128)(2,1)}, u32[]{:S(2)}, u32[]{:S(2)}) collective-permute-start(bf16[256,256]{1,0:T(8,128)(2,1)} %collective-permute-done.42), channel_id=1, source_target_pairs={{0,1},{1,2},{2,3},{3,4},{4,5},{5,6},{6,7},{7,8},{8,9},{9,10},{10,1... | collective-permute-start | bytes 393224 | tf_op jit(solution)/shard_map/ppermute | solution.py:13
  227.1 131.9 %all-reduce.9.cloned.1.call-start = ((), (), s32[]{:S(2)}) async-start(), calls=%async_computation.2 | async-start | bytes 786432 | tf_op jit(solution)/shard_map/psum | solution.py:25
  227.2 143.3 %collective-permute-start.59 = (bf16[256,256]{1,0:T(8,128)(2,1)S(1)}, bf16[256,256]{1,0:T(8,128)(2,1)S(1)}, u32[]{:S(2)}, u32[]{:S(2)}) collective-permute-start(bf16[256,256]{1,0:T(8,128)(2,1)S(1)} %collective-permute-done.57), channel_id=1, source_target_pairs={{0,1},{1,2},{2,3},{3,4},{4,5},{5,6},{6,7},{7,8},{8,9},{9,10},{10,1... | collective-permute-start | bytes 393224 | tf_op jit(solution)/shard_map/ppermute | solution.py:13
  299.1 130.6 %all-reduce.11.cloned.1.call-start = ((), (), s32[]{:S(2)}) async-start(), calls=%async_computation.3 | async-start | bytes 786432 | tf_op jit(solution)/shard_map/psum | solution.py:25
  (8 other events, 36.5 us)
Sparse Core Ops, SparseCore 0:
  22.4 57.4 all-reduce.4
  227.2 61.6 all-reduce.6
  299.2 59.7 all-reduce.8
  369.9 59.7 all-reduce.10
